TPU v7x, 256 devices: a whole 4x4x8 slice. The times are simulated.
256 devices in a mesh: pair: 8 (over y_lo, x), feat: 32 (over y_hi, z, core).
Axes of the slice: x: 4, y: 4 (y_hi: 2, y_lo: 2; y = y_hi * 2 + y_lo), z: 8, core: 2. Of those that a mesh axis runs over, the one named last changes fastest.
Arguments:
- decoder: float32 [8, 16384, 2048], P('pair', 'feat'), may hold values from -0.3125 to 0.3125
- pair_map: int32 [8, 2], P('pair'), may hold values from 0 to 3, as said below
- indices: int32 [3, 256, 128], replicated, may hold values from 0 to 16383, as said below
- values: float32 [3, 256, 128], replicated, may hold values from 0.2 to 3
- target: float32 [3, 256, 2048], P(None, ('pair', 'feat')), may hold values from -6 to 6
Outputs:
- recon: bfloat16 [3, 256, 2048], P(None, ('pair', 'feat'))
- dec_grad: float32 [8, 16384, 2048], P('pair', 'feat')
- feat_grad: float32 [3, 256, 128], P(None, ('pair', 'feat'))
Inputs may be any that keep to these rules, and one draw needn't show every extreme that they name: `pair_map`: each pair (s, t) of layers with s <= t < 3 stands in exactly one row as (s, t); every other row is (3, 3), an empty slot. For each layer and token the 128 indices are distinct.
All inputs are finite; a program needn't handle non-finite values.
Results may differ from a plain program's by a relative error of at most 0.0027.
Values may be sent and summed in bfloat16 or wider, within the bound.
A program may use at most 128 MiB of HBM per device.

v0:
```python
import jax
import jax.numpy as jnp
from jax import lax
from jax.sharding import PartitionSpec as P


def pick_layer(stack, chosen_layer):
    layer_ids = jnp.arange(stack.shape[0], dtype=jnp.int32)[:, None, None]
    return jnp.sum(jnp.where(layer_ids == chosen_layer, stack, jnp.zeros_like(stack)), axis=0)


def body(decoder, pair_map, indices, values, target):
    slot_count, block_width, model_width = decoder.shape
    layers = indices.shape[0]
    first_feature = lax.axis_index("feat") * block_width
    columns = jnp.arange(block_width, dtype=jnp.int32)
    sources = pair_map[:, 0]
    goals = pair_map[:, 1]
    slot_index = 0
    picked = jnp.minimum(sources[slot_index], layers - 1)
    local_ids = pick_layer(indices, picked) - first_feature
    weights = pick_layer(values, picked)
    matches = (local_ids[:, :, None] == columns).astype(jnp.float32)
    active = jnp.einsum(
        "tk,tkf->tf",
        weights,
        matches,
        precision=lax.Precision.HIGHEST,
        preferred_element_type=jnp.float32,
    )
    product = jnp.dot(
        active,
        decoder[slot_index],
        precision=lax.Precision.HIGHEST,
        preferred_element_type=jnp.float32,
    )
    local_list = [local_ids]
    active_list = [active]
    product_list = [product]
    stacked = jnp.stack(product_list)
    choose_goal = jax.nn.one_hot(goals, layers, dtype=jnp.float32)
    choose_narrow = choose_goal.astype(jnp.bfloat16)
    layer_term = jnp.einsum(
        "jl,jtd->ltd",
        choose_goal,
        stacked,
        precision=lax.Precision.HIGHEST,
        preferred_element_type=jnp.float32,
    )
    shares = lax.psum_scatter(layer_term, ("pair", "feat"), scatter_dimension=1, tiled=True)
    error_share = (shares - target).astype(jnp.bfloat16)
    error_full = lax.all_gather(error_share, ("pair", "feat"), axis=1, tiled=True)
    slot_errors = jnp.einsum(
        "jl,ltd->jtd", choose_narrow, error_full, preferred_element_type=jnp.float32
    ).astype(jnp.bfloat16)
    recon = shares.astype(jnp.bfloat16)
    slot_index = 0
    slot_error = slot_errors[slot_index].astype(jnp.float32)
    tile_grad = jnp.dot(
        active_list[slot_index].T,
        slot_error,
        precision=lax.Precision.HIGHEST,
        preferred_element_type=jnp.float32,
    )
    grad_list = [tile_grad]
    back = jnp.dot(
        slot_error,
        decoder[slot_index].T,
        precision=lax.Precision.HIGHEST,
        preferred_element_type=jnp.float32,
    )
    matches = (local_list[slot_index][:, :, None] == columns).astype(jnp.float32)
    picked_grad = jnp.einsum(
        "tkf,tf->tk",
        matches,
        back,
        precision=lax.Precision.HIGHEST,
        preferred_element_type=jnp.float32,
    )
    choose_source = jax.nn.one_hot(sources[slot_index], layers, dtype=jnp.float32)
    feature_term = choose_source[:, None, None] * picked_grad[None]
    dec_grad = jnp.stack(grad_list)
    feat_grad = lax.psum_scatter(feature_term, ("pair", "feat"), scatter_dimension=1, tiled=True)
    return (recon, dec_grad, feat_grad)


def solution(mesh):
    in_specs = (P("pair", "feat", None), P("pair", None), P(), P(), P(None, ("pair", "feat"), None))
    out_specs = (
        P(None, ("pair", "feat"), None),
        P("pair", "feat", None),
        P(None, ("pair", "feat"), None),
    )
    return jax.shard_map(body, mesh=mesh, in_specs=in_specs, out_specs=out_specs, check_vma=False)
```

profile of v0, /device:TPU:2, one launch (start us, length us, event | category | flops | bytes accessed | tf_op | source)
XLA Modules:
  0.0 1048.4 jit_solution(10654120748516346442)
XLA Ops:
  7.2 0.0 all-reduce.5.cloned.1.call-start
  7.2 1.3 fusion.18
  9.2 1.1 select_reduce_fusion
  10.3 1.1 select_reduce_fusion.1
  11.4 0.7 compare_convert_fusion.1
  12.1 0.0 copy-start
  12.1 23.2 %fusion.1 = f32[256,1,512]{2,1,0:T(1,128)S(1)} fusion(f32[256,128,1]{1,2,0:T(1,128)S(1)} %bitcast.32, s32[256,128]{1,0:T(8,128)S(1)} %broadcast_subtract_fusion), kind=kOutput, calls=%fused_computation.2 | convolution fusion | flops 218103808 | bytes 786432 | tf_op jit(solution)/shard_map/tk,tkf->tf/dot_general | solution.py:24
  35.3 0.0 copy-done
  35.3 3.7 fusion.6
  39.0 5.7 broadcast_multiply_fusion
  44.7 0.0 copy-start.2
  44.7 0.0 all-reduce.5.cloned.1.call-update
  44.7 0.0 all-gather.2.cloned.1.call-start
  44.8 283.0 %all-reduce.5.cloned.1.call-done = f32[3,256,2048]{2,0,1:T(4,128)} async-done(((f32[3,256,2048]{2,0,1:T(4,128)}), f32[3,256,2048]{2,0,1:T(4,128)}) %all-reduce.5.cloned.1.call-update) | async-done | bytes 6291472
  327.8 0.0 copy-done.2
  327.8 1.4 fusion.16
  329.2 0.0 all-gather.2.cloned.1.call-update
  329.2 0.2 all-reduce.7.cloned.1.call-start
  329.5 0.7 compare_convert_fusion
  330.1 1.4 dynamic-slice_convert_fusion
  331.5 414.0 %all-gather.2.cloned.1.call-done = bf16[3,256,2048]{2,0,1:T(4,128)(2,1)} async-done(((bf16[3,1,2048]{2,0,1:T(4,128)(2,1)}), bf16[3,256,2048]{2,0,1:T(4,128)(2,1)}) %all-gather.2.cloned.1.call-update) | async-done | bytes 3145744 | tf_op jit(solution)/shard_map/all_gather | solution.py:52
  745.5 0.0 copy-start.1
  745.5 5.5 fusion.17
  750.9 0.0 copy-done.1
  750.9 2.6 fusion.8
  753.5 32.3 %fusion = f32[256,1,128]{2,1,0:T(1,128)S(1)} fusion(s32[256,128]{1,0:T(8,128)S(1)} %broadcast_subtract_fusion, f32[256,512,1]{1,0,2:T(8,128)S(1)} %fusion.8), kind=kOutput, calls=%fused_computation.1 | convolution fusion | flops 218103808 | bytes 786432 | tf_op jit(solution)/shard_map/tkf,tf->tk/dot_general | solution.py:73
  785.9 1.0 broadcast_multiply_fusion.1
  786.8 0.0 all-reduce.7.cloned.1.call-update
  786.9 4.1 convolution_bitcast_fusion
  791.0 249.6 %all-reduce.7.cloned.1.call-done = f32[3,256,128]{2,0,1:T(4,128)} async-done(((f32[3,256,128]{2,0,1:T(4,128)}), f32[3,256,128]{2,0,1:T(4,128)}) %all-reduce.7.cloned.1.call-update) | async-done | bytes 393232
  1040.6 0.7 constant_dynamic-slice_fusion
  1041.3 0.6 copy.10
  (2 shorter events, 0.0 us)
Async XLA Ops:
  7.2 320.7 %all-reduce.5.cloned.1.call-start = ((), (), s32[]{:S(2)}) async-start(), calls=%async_computation.1 | async-start | bytes 16777216
  12.1 23.2 %copy-start = (f32[1,512,2048]{2,1,0:T(8,128)S(1)}, f32[1,512,2048]{2,1,0:T(8,128)}, u32[]{:S(2)}) copy-start(f32[1,512,2048]{2,1,0:T(8,128)} %param.5) | copy-start | bytes 12582916
  44.7 283.1 %copy-start.2 = (f32[3,1,2048]{2,1,0:T(1,128)S(1)}, f32[3,1,2048]{2,1,0:T(1,128)}, u32[]{:S(2)}) copy-start(f32[3,1,2048]{2,1,0:T(1,128)} %param.9) | copy-start | bytes 73732
  44.7 700.7 %all-gather.2.cloned.1.call-start = ((), (), s32[]{:S(2)}) async-start(), calls=%async_computation | async-start | bytes 4210688 | tf_op jit(solution)/shard_map/all_gather | solution.py:52
  329.2 711.3 %all-reduce.7.cloned.1.call-start = ((), (), s32[]{:S(2)}) async-start(), calls=%async_computation.2 | async-start | bytes 1048576
  745.5 5.5 copy-start.1
Sparse Core Ops, SparseCore 0:
  44.8 282.9 all-reduce.4
  330.3 415.1 all-gather.1
  787.0 253.5 all-reduce.6
where the time goes:
time: 1050 us
  waiting for transfers between devices  947 us (90%)
  matrix products  71.4 us (7%)
  between operations  14.5 us (1%)
  other arithmetic  11.5 us (1%)
    unnamed x5, waiting for transfers between devices  533 us
    all_gather x1, waiting for transfers between devices, body(): lax.all_gather(error_share, ('pair', 'feat'), axis=1, tiled=True)  414 us
    dot_general x1, matrix products, body(): jnp.einsum('tkf,tf->tk', matches, back, precision=lax.Precision.HIGHEST,...  32.3 us
    dot_general x1, matrix products, body(): jnp.einsum('tk,tkf->tf', weights, matches, precision=lax.Precision.HIGHES...  23.2 us
  transfers between devices with their start and end apart: 3, of which 3 were waited for; matrix products, arithmetic and copies ran while one was open for 1% of the time, Pallas kernels for 0%

commit v1 on v0

--- a/solution.py
+++ b/solution.py
@@ -49,7 +49,12 @@
     )
     shares = lax.psum_scatter(layer_term, ("pair", "feat"), scatter_dimension=1, tiled=True)
     error_share = (shares - target).astype(jnp.bfloat16)
-    error_full = lax.all_gather(error_share, ("pair", "feat"), axis=1, tiled=True)
+    error_full = jnp.concatenate(
+        lax.all_to_all(
+            jnp.stack([error_share] * lax.axis_size(("pair", "feat"))), ("pair", "feat"), 0, 0
+        ),
+        axis=1,
+    )
     slot_errors = jnp.einsum(
         "jl,ltd->jtd", choose_narrow, error_full, preferred_element_type=jnp.float32
     ).astype(jnp.bfloat16)

time: 1050 us -> 744 us (0.71)
  waiting for transfers between devices: 947 us -> 624 us
  starting transfers between devices: 0.3 us -> 11.8 us
    all_gather x1 -> x0, waiting for transfers between devices: 414 us -> none  [body(): lax.all_gather(error_share, ('pair', 'feat'), axis=1, tiled=True)]
    all_to_all x0 -> x1, waiting for transfers between devices: none -> 91.9 us  [body(): lax.all_to_all(jnp.stack([error_share] * lax.axis_size(('pair', 'feat')))...]
    all_to_all x0 -> x1, starting transfers between devices: none -> 11.5 us  [body(): lax.all_to_all(jnp.stack([error_share] * lax.axis_size(('pair', 'feat')))...]
    unnamed x5 -> x4, waiting for transfers between devices: 533 us -> 532 us
where the time goes in v1:
time: 744 us
  waiting for transfers between devices  624 us (84%)
  matrix products  69.8 us (9%)
  between operations  14.8 us (2%)
  local copies, waits for them, and re-layouts  12.5 us (2%)
  starting transfers between devices  11.8 us (2%)
  other arithmetic  10.9 us (1%)
    unnamed x4, waiting for transfers between devices  532 us
    all_to_all x1, waiting for transfers between devices, body(): lax.all_to_all(jnp.stack([error_share] * lax.axis_size(('pair', 'feat')))...  91.9 us
    dot_general x1, matrix products, body(): jnp.einsum('tkf,tf->tk', matches, back, precision=lax.Precision.HIGHEST,...  32.3 us
    dot_general x1, matrix products, body(): jnp.einsum('tk,tkf->tf', weights, matches, precision=lax.Precision.HIGHES...  23.2 us
  transfers between devices with their start and end apart: 3, of which 3 were waited for; matrix products, arithmetic and copies ran while one was open for 1% of the time, Pallas kernels for 0%

profile of v1, /device:TPU:2, one launch (start us, length us, event | category | flops | bytes accessed | tf_op | source)
XLA Modules:
  0.0 744.0 jit_solution(3360325042315136653)
XLA Ops:
  7.2 0.0 all-reduce.5.cloned.1.call-start
  7.2 1.3 fusion.25
  9.2 1.1 select_reduce_fusion.1
  10.3 1.1 select_reduce_fusion
  11.4 0.7 compare_convert_fusion.2
  12.1 0.0 copy-start
  12.1 23.2 %fusion.1 = f32[256,1,512]{2,1,0:T(1,128)S(1)} fusion(f32[256,128,1]{1,2,0:T(1,128)S(1)} %bitcast.41, s32[256,128]{1,0:T(8,128)S(1)} %broadcast_subtract_fusion), kind=kOutput, calls=%fused_computation.2 | convolution fusion | flops 218103808 | bytes 786432 | tf_op jit(solution)/shard_map/tk,tkf->tf/dot_general | solution.py:24
  35.3 0.0 copy-done
  35.3 3.7 fusion.6
  39.0 5.7 broadcast_multiply_fusion
  44.7 0.0 copy-start.2
  44.7 0.0 all-reduce.5.cloned.1.call-update
  44.7 283.1 %all-reduce.5.cloned.1.call-done = f32[3,256,2048]{2,0,1:T(4,128)} async-done(((f32[3,256,2048]{2,0,1:T(4,128)}), f32[3,256,2048]{2,0,1:T(4,128)}) %all-reduce.5.cloned.1.call-update) | async-done | bytes 6291472
  327.8 0.0 copy-done.2
  327.8 0.8 fusion.19
  328.6 4.1 stack.4
  332.7 11.5 %all-to-all-start = ((bf16[256,3,1,2048]{3,1,2,0:T(4,128)(2,1)}), bf16[256,3,1,2048]{3,1,2,0:T(4,128)(2,1)}, u32[]{:S(2)}, u32[]{:S(2)}) async-start(bf16[256,3,1,2048]{3,1,2,0:T(4,128)(2,1)} %stack.4), calls=%async_computation | async-start | bytes 8388608 | tf_op jit(solution)/shard_map/all_to_all | solution.py:53
  344.3 0.2 all-reduce.7.cloned.1.call-start
  344.5 0.7 compare_convert_fusion
  345.2 1.4 dynamic-slice_convert_fusion
  346.6 91.9 %all-to-all-done = bf16[256,3,1,2048]{3,1,2,0:T(4,128)(2,1)} async-done(((bf16[256,3,1,2048]{3,1,2,0:T(4,128)(2,1)}), bf16[256,3,1,2048]{3,1,2,0:T(4,128)(2,1)}, u32[]{:S(2)}, u32[]{:S(2)}) %all-to-all-start) | async-done | bytes 3145760 | tf_op jit(solution)/shard_map/all_to_all | solution.py:53
  438.5 4.5 copy.41
  442.9 0.0 copy-start.1
  442.9 3.8 fusion.8
  446.7 0.0 copy-done.1
  446.7 2.6 fusion.10
  449.3 32.3 %fusion = f32[256,1,128]{2,1,0:T(1,128)S(1)} fusion(s32[256,128]{1,0:T(8,128)S(1)} %broadcast_subtract_fusion, f32[256,512,1]{1,0,2:T(8,128)S(1)} %fusion.10), kind=kOutput, calls=%fused_computation.1 | convolution fusion | flops 218103808 | bytes 786432 | tf_op jit(solution)/shard_map/tkf,tf->tk/dot_general | solution.py:78
  481.7 1.0 broadcast_multiply_fusion.1
  482.7 0.0 all-reduce.7.cloned.1.call-update
  482.7 4.1 convolution_bitcast_fusion
  486.8 249.1 %all-reduce.7.cloned.1.call-done = f32[3,256,128]{2,0,1:T(4,128)} async-done(((f32[3,256,128]{2,0,1:T(4,128)}), f32[3,256,128]{2,0,1:T(4,128)}) %all-reduce.7.cloned.1.call-update) | async-done | bytes 393232
  735.9 0.7 constant_dynamic-slice_fusion
  736.6 0.6 copy.12
  (2 shorter events, 0.0 us)
Async XLA Ops:
  7.2 320.7 %all-reduce.5.cloned.1.call-start = ((), (), s32[]{:S(2)}) async-start(), calls=%async_computation.1 | async-start | bytes 16777216
  12.1 23.2 %copy-start = (f32[1,512,2048]{2,1,0:T(8,128)S(1)}, f32[1,512,2048]{2,1,0:T(8,128)}, u32[]{:S(2)}) copy-start(f32[1,512,2048]{2,1,0:T(8,128)} %param.5) | copy-start | bytes 12582916
  44.7 283.1 %copy-start.2 = (f32[3,1,2048]{2,1,0:T(1,128)S(1)}, f32[3,1,2048]{2,1,0:T(1,128)}, u32[]{:S(2)}) copy-start(f32[3,1,2048]{2,1,0:T(1,128)} %param.9) | copy-start | bytes 73732
  332.7 105.7 %all-to-all-start = ((bf16[256,3,1,2048]{3,1,2,0:T(4,128)(2,1)}), bf16[256,3,1,2048]{3,1,2,0:T(4,128)(2,1)}, u32[]{:S(2)}, u32[]{:S(2)}) async-start(bf16[256,3,1,2048]{3,1,2,0:T(4,128)(2,1)} %stack.4), calls=%async_computation | async-start | bytes 8388608 | tf_op jit(solution)/shard_map/all_to_all | solution.py:53
  344.3 391.6 %all-reduce.7.cloned.1.call-start = ((), (), s32[]{:S(2)}) async-start(), calls=%async_computation.2 | async-start | bytes 1048576
  442.9 3.8 copy-start.1
Sparse Core Ops, SparseCore 0:
  44.8 282.9 all-reduce.4
  482.8 253.0 all-reduce.6
